TPU v7x, 128 devices: a whole 4x4x4 slice. The times are simulated.
128 devices in a mesh: row: 8 (over z, core), col: 16 (over y, x).
Axes of the slice: x: 4, y: 4, z: 4, core: 2. Of those that a mesh axis runs over, the one named last changes fastest.
Arguments:
- fock: bfloat16 [18432, 18432], P('row', 'col'), may hold values from -6 to 6
- intersection: bfloat16 [18432, 18432], P('row', 'col'), may hold values from -6 to 6
- tile_mask: int32 [2, 144, 144], P(None, 'row', 'col'), may hold values 0 or 1
- coefficients: bfloat16 [256, 7, 20, 128], P(('row', 'col')), may hold values from -0.5 to 0.5
- domains: int32 [256, 7], P(('row', 'col')), may hold values from 0 to 143, all different within a row; in each aligned block of 32 rows (0 to 31, 32 to 63, ...) at most 2 rows name the same one
- neighbours: int32 [256, 2], P(('row', 'col')), may hold values from 0 to 255, all different within a row
- amplitudes: float32 [256, 20, 20], P(('row', 'col')), may hold values from -0.18 to 0.18
Outputs:
- projected: float32 [256, 20, 20], P(('row', 'col'))
Inputs may be any that keep to these rules, and one draw needn't show every extreme that they name: `domains`: each pair names 7 different tiles; among the 32 pairs of one row index (an aligned block of pairs) no tile is named by more than 2 slots. `neighbours`: each pair names 2 different pairs.
All inputs are finite; a program needn't handle non-finite values. No bound on the sum of `tile_mask` on one device may be relied on, other than what follows from the above.
Results may differ from a plain program's by a relative error of at most 0.0041.
Values may be sent and summed in bfloat16 or wider, within the bound.
A program may use at most 256 MiB of HBM per device.

v0:
```python
import jax
import jax.numpy as jnp
from jax import lax
from jax.sharding import PartitionSpec as P

HIGH = lax.Precision.HIGHEST


def in_one_piece(arrays, axis, dim, along):
    both = jnp.concatenate(arrays, axis=along)
    whole, at, done = (lax.all_gather(both, axis, axis=dim, tiled=True), 0, [])
    for a in arrays:
        done.append(lax.slice_in_dim(whole, at, at + a.shape[along], axis=along))
        at += a.shape[along]
    return tuple(done)


def split_up(x, dim, length):
    dims = x.shape
    tiles = x.reshape(*dims[:dim], length, dims[dim] // length, *dims[dim + 1 :])
    return jnp.moveaxis(tiles, dim, 0)


def sent_and_summed(x, axis, dim):
    tiles = split_up(x, dim, lax.axis_size(axis))
    arrived = lax.all_to_all(tiles, axis, split_axis=0, concat_axis=0, tiled=True)
    return arrived.sum(axis=0)


def bucket_slots(coeffs, tiles, base_pair, first_tile, tile_count, capacity):
    group_size, per_pair = tiles.shape
    slot_count = group_size * per_pair
    flat_tiles = tiles.reshape(slot_count)
    position = jnp.arange(slot_count, dtype=jnp.int32)
    pair_owner = base_pair + position // per_pair
    earlier = (flat_tiles[:, None] == flat_tiles[None, :]) & (position[None, :] < position[:, None])
    slot_rank = jnp.sum(earlier.astype(jnp.int32), axis=1)
    wanted = first_tile + jnp.arange(tile_count, dtype=jnp.int32)
    levels = jnp.arange(capacity, dtype=jnp.int32)
    matches = (flat_tiles[None, None, :] == wanted[:, None, None]) & (
        slot_rank[None, None, :] == levels[None, :, None]
    )
    present = jnp.any(matches, axis=2)
    source = jnp.sum(matches.astype(jnp.int32) * position[None, None, :], axis=2)
    flat_coeffs = coeffs.reshape((slot_count,) + coeffs.shape[2:])
    blocks = jnp.take(flat_coeffs, source, axis=0)
    blocks = jnp.where(present[:, :, None, None], blocks, jnp.zeros((), blocks.dtype))
    owners = jnp.where(present, jnp.take(pair_owner, source), -1)
    return (blocks, owners)


def shards(fock, intersection, tile_mask, coefficients, domains, neighbours, amplitudes):
    row_count = lax.axis_size("row")
    col_count = lax.axis_size("col")
    row_index = lax.axis_index("row")
    col_index = lax.axis_index("col")
    pair_dev, per_pair, pno_count, tile_size = coefficients.shape
    link_count = neighbours.shape[1]
    tile_rows = fock.shape[0] // tile_size
    tile_cols = fock.shape[1] // tile_size
    capacity = max(2, pair_dev)
    group_size = pair_dev * col_count
    width = fock.shape[1]
    group_coeffs, group_tiles, group_links = (
        lax.all_gather(coefficients, "col", axis=0, tiled=True),
        *in_one_piece((domains, neighbours), "col", 0, 1),
    )

    def rows_of(coeffs, tiles, base_pair):
        return bucket_slots(coeffs, tiles, base_pair, row_index * tile_rows, tile_rows, capacity)

    def cols_of(coeffs, tiles, base_pair):
        return bucket_slots(coeffs, tiles, base_pair, col_index * tile_cols, tile_cols, capacity)

    all_coeffs, all_tiles, all_links = (
        lax.all_gather(group_coeffs, "row", axis=0, tiled=True),
        lax.all_gather(group_tiles, "row", axis=0, tiled=True),
        lax.all_gather(group_links, "row", axis=0, tiled=True),
    )
    grouped_coeffs = all_coeffs.reshape((row_count, group_size) + all_coeffs.shape[1:])
    grouped_tiles = all_tiles.reshape(row_count, group_size, per_pair)
    bases = jnp.arange(row_count, dtype=jnp.int32) * group_size
    row_blocks, row_owners = jax.vmap(rows_of)(grouped_coeffs, grouped_tiles, bases)
    col_blocks, col_owners = jax.vmap(cols_of)(grouped_coeffs, grouped_tiles, bases)

    def masked(matrix, flags):
        tiled = matrix.reshape(tile_rows, tile_size, tile_cols, tile_size)
        return (tiled * flags.astype(matrix.dtype)[:, None, :, None]).reshape(matrix.shape)

    operator = jnp.concatenate(
        [masked(fock, tile_mask[0]), masked(intersection, tile_mask[1])], axis=1
    )
    operator = operator.reshape(tile_rows, tile_size, 2 * width)
    link_groups = all_links.reshape(row_count, group_size, link_count)
    group_bases = jnp.arange(row_count, dtype=jnp.int32) * group_size

    def one_group(inputs):
        blocks, owners, links_here, base_pair = inputs
        parts = jnp.einsum("tmak,tkw->tmaw", blocks, operator, preferred_element_type=jnp.float32)
        members = base_pair + jnp.arange(group_size, dtype=jnp.int32)
        flat_owners = owners.reshape(-1)
        bucket_count = flat_owners.shape[0]
        flat_parts = parts.reshape(bucket_count, pno_count, 2 * width)
        hits = flat_owners[None, :] == members[:, None]
        order = jnp.cumsum(hits.astype(jnp.int32), axis=1) - 1
        spots = jnp.arange(bucket_count, dtype=jnp.int32)
        total = jnp.zeros((group_size, pno_count, 2 * width), jnp.float32)
        for slot in range(per_pair):
            pick = hits & (order == slot)
            found = jnp.any(pick, axis=1)
            where_at = jnp.sum(pick.astype(jnp.int32) * spots[None, :], axis=1)
            picked = jnp.take(flat_parts, where_at, axis=0)
            total = total + jnp.where(found[:, None, None], picked, jnp.zeros((), jnp.float32))
        left = total.astype(jnp.bfloat16)
        left = left.reshape(group_size, pno_count, 2, tile_cols, tile_size)
        chosen = (col_owners[None, None] == links_here[:, :, None, None, None]).astype(jnp.bfloat16)
        partner = jnp.einsum(
            "qngtm,gtmbk->qntbk", chosen, col_blocks, preferred_element_type=jnp.float32
        ).astype(jnp.bfloat16)
        return jnp.einsum("qamtk,qntbk->qnmab", left, partner, preferred_element_type=jnp.float32)

    terms = lax.map(one_group, (row_blocks, row_owners, link_groups, group_bases))
    flat_terms = terms.reshape(row_count * group_size, -1)
    sectioned = flat_terms.reshape(row_count, col_count, pair_dev, -1)
    sectioned = sent_and_summed(sectioned, "col", 1)
    summed = sent_and_summed(sectioned, "row", 0)
    summed = summed.reshape(pair_dev, link_count, 2, pno_count, pno_count)
    every_amp = lax.all_gather(amplitudes, ("row", "col"), axis=0, tiled=True)
    nearby = jnp.take(every_amp, neighbours, axis=0)
    fock_part = summed[:, :, 0]
    over_part = summed[:, :, 1]
    first = jnp.einsum("pnab,pnbc,pndc->pad", over_part, nearby, fock_part, precision=HIGH)
    second = jnp.einsum("pnab,pnbc,pndc->pad", fock_part, nearby, over_part, precision=HIGH)
    return first + second


def solution(mesh):
    placed = (
        P("row", "col"),
        P("row", "col"),
        P(None, "row", "col"),
        P(("row", "col"), None, None, None),
        P(("row", "col"), None),
        P(("row", "col"), None),
        P(("row", "col"), None, None),
    )
    return jax.shard_map(
        shards, mesh=mesh, in_specs=placed, out_specs=P(("row", "col"), None, None), check_vma=False
    )
```

profile of v0, /device:TPU:1, one launch (start us, length us, event | category | flops | bytes accessed | tf_op | source)
XLA Modules:
  0.0 1144.9 jit_solution(11759695750382023470)
XLA Ops:
  8.1 45.8 %all-gather.6.cloned.1.call-done = bf16[32,7,20,128]{3,1,2,0:T(8,128)(2,1)} async-done(((bf16[2,7,20,128]{3,1,2,0:T(8,128)(2,1)}), bf16[32,7,20,128]{3,1,2,0:T(8,128)(2,1)}) %all-gather.6.cloned.1.call-update) | async-done | bytes 1146896 | tf_op jit(solution)/shard_map/all_gather | solution.py:65
  57.5 17.6 %all-gather = s32[16,2,9]{2,1,0:T(2,128)S(1)} all-gather(s32[1,2,9]{2,1,0:T(2,128)S(1)} %add_bitcast_fusion), channel_id=1, replica_groups=mesh['row'=8,'col'=16] {'col'}, dimensions={0}, use_global_device_ids=true | all-gather | bytes 1224 | tf_op jit(solution)/shard_map/all_gather | solution.py:11
  75.3 21.1 %all-gather.1 = s32[8,32,7]{1,2,0:T(8,128)S(1)} all-gather(s32[1,32,7]{1,2,0:T(8,128)S(1)} %bitcast.147), channel_id=1, replica_groups=mesh['row'=8,'col'=16] {'row'}, dimensions={0}, use_global_device_ids=true | all-gather | bytes 8064 | tf_op jit(solution)/shard_map/all_gather | solution.py:77
  154.9 11.4 all-gather.2
  166.8 9.3 pad_maximum_fusion
  176.0 13.8 %copy.171 = bf16[256,7,20,128]{3,2,1,0:T(8,128)(2,1)} copy(bf16[256,7,20,128]{3,0,2,1:T(8,128)(2,1)} %all-gather.8.cloned.1.call-done) | data formatting | bytes 18350080 | tf_op jit(solution)/shard_map/vmap()/reshape;reshape | solution.py:45
  206.4 815.7 %while.12 = (s32[]{:T(128)}, f32[8,32,2,2,20,20]{5,4,3,2,0,1:T(8,128)}, s32[8,9,2]{0,2,1:T(2,128)S(1)}, s32[8,32,2]{1,2,0:T(2,128)}, bf16[8,9,2,20,128]{4,0,2,3,...) while((s32[]{:T(128)}, ...), condition=%wide.region_21.23_spmd, body=%wide.region_5.22_spmd.sunk | while | flops 622367552 | bytes 162233904 | solution.py:122
  220.1 8.9 fusion.72
  281.2 18.9 %fusion.74 = bf16[32,20,2304]{2,1,0:T(8,128)(2,1)S(1)} fusion(f32[32,20,2304]{2,1,0:T(8,128)} %gather_fusion, f32[32,20,2304]{2,1,0:T(8,128)} %gather_fusion.1, f32[32,20,2304]{2,1,0:T(8,128)} %gather_fusion.2, f32[32,20,2304]{2,1,0:T(8,128)} %gather_fusion.3, f32[32,20,2304]{2,1,0:T(8,128)} %gather_fusion.4, f32[32,20,2304]{2,1,0:T(8,128)} %gather_fusion.5, ...), kind=kLoop, calls=%fused_computation.16.clone.1 | loop fusion | flops 30965760 | bytes 44237248 | tf_op jit(solution)/shard_map/while/body/eval_jaxpr/convert_element_type | solution.py:114
  320.9 8.9 fusion.72
  381.9 18.9 %fusion.74 = bf16[32,20,2304]{2,1,0:T(8,128)(2,1)S(1)} fusion(f32[32,20,2304]{2,1,0:T(8,128)} %gather_fusion, f32[32,20,2304]{2,1,0:T(8,128)} %gather_fusion.1, f32[32,20,2304]{2,1,0:T(8,128)} %gather_fusion.2, f32[32,20,2304]{2,1,0:T(8,128)} %gather_fusion.3, f32[32,20,2304]{2,1,0:T(8,128)} %gather_fusion.4, f32[32,20,2304]{2,1,0:T(8,128)} %gather_fusion.5, ...), kind=kLoop, calls=%fused_computation.16.clone.1 | loop fusion | flops 30965760 | bytes 44237248 | tf_op jit(solution)/shard_map/while/body/eval_jaxpr/convert_element_type | solution.py:114
  421.6 8.9 fusion.72
  482.6 18.9 %fusion.74 = bf16[32,20,2304]{2,1,0:T(8,128)(2,1)S(1)} fusion(f32[32,20,2304]{2,1,0:T(8,128)} %gather_fusion, f32[32,20,2304]{2,1,0:T(8,128)} %gather_fusion.1, f32[32,20,2304]{2,1,0:T(8,128)} %gather_fusion.2, f32[32,20,2304]{2,1,0:T(8,128)} %gather_fusion.3, f32[32,20,2304]{2,1,0:T(8,128)} %gather_fusion.4, f32[32,20,2304]{2,1,0:T(8,128)} %gather_fusion.5, ...), kind=kLoop, calls=%fused_computation.16.clone.1 | loop fusion | flops 30965760 | bytes 44237248 | tf_op jit(solution)/shard_map/while/body/eval_jaxpr/convert_element_type | solution.py:114
  522.4 8.9 fusion.72
  583.4 18.9 %fusion.74 = bf16[32,20,2304]{2,1,0:T(8,128)(2,1)S(1)} fusion(f32[32,20,2304]{2,1,0:T(8,128)} %gather_fusion, f32[32,20,2304]{2,1,0:T(8,128)} %gather_fusion.1, f32[32,20,2304]{2,1,0:T(8,128)} %gather_fusion.2, f32[32,20,2304]{2,1,0:T(8,128)} %gather_fusion.3, f32[32,20,2304]{2,1,0:T(8,128)} %gather_fusion.4, f32[32,20,2304]{2,1,0:T(8,128)} %gather_fusion.5, ...), kind=kLoop, calls=%fused_computation.16.clone.1 | loop fusion | flops 30965760 | bytes 44237248 | tf_op jit(solution)/shard_map/while/body/eval_jaxpr/convert_element_type | solution.py:114
  623.1 8.9 fusion.72
  684.1 18.9 %fusion.74 = bf16[32,20,2304]{2,1,0:T(8,128)(2,1)S(1)} fusion(f32[32,20,2304]{2,1,0:T(8,128)} %gather_fusion, f32[32,20,2304]{2,1,0:T(8,128)} %gather_fusion.1, f32[32,20,2304]{2,1,0:T(8,128)} %gather_fusion.2, f32[32,20,2304]{2,1,0:T(8,128)} %gather_fusion.3, f32[32,20,2304]{2,1,0:T(8,128)} %gather_fusion.4, f32[32,20,2304]{2,1,0:T(8,128)} %gather_fusion.5, ...), kind=kLoop, calls=%fused_computation.16.clone.1 | loop fusion | flops 30965760 | bytes 44237248 | tf_op jit(solution)/shard_map/while/body/eval_jaxpr/convert_element_type | solution.py:114
  723.9 8.9 fusion.72
  784.9 18.9 %fusion.74 = bf16[32,20,2304]{2,1,0:T(8,128)(2,1)S(1)} fusion(f32[32,20,2304]{2,1,0:T(8,128)} %gather_fusion, f32[32,20,2304]{2,1,0:T(8,128)} %gather_fusion.1, f32[32,20,2304]{2,1,0:T(8,128)} %gather_fusion.2, f32[32,20,2304]{2,1,0:T(8,128)} %gather_fusion.3, f32[32,20,2304]{2,1,0:T(8,128)} %gather_fusion.4, f32[32,20,2304]{2,1,0:T(8,128)} %gather_fusion.5, ...), kind=kLoop, calls=%fused_computation.16.clone.1 | loop fusion | flops 30965760 | bytes 44237248 | tf_op jit(solution)/shard_map/while/body/eval_jaxpr/convert_element_type | solution.py:114
  824.6 8.9 fusion.72
  885.6 18.9 %fusion.74 = bf16[32,20,2304]{2,1,0:T(8,128)(2,1)S(1)} fusion(f32[32,20,2304]{2,1,0:T(8,128)} %gather_fusion, f32[32,20,2304]{2,1,0:T(8,128)} %gather_fusion.1, f32[32,20,2304]{2,1,0:T(8,128)} %gather_fusion.2, f32[32,20,2304]{2,1,0:T(8,128)} %gather_fusion.3, f32[32,20,2304]{2,1,0:T(8,128)} %gather_fusion.4, f32[32,20,2304]{2,1,0:T(8,128)} %gather_fusion.5, ...), kind=kLoop, calls=%fused_computation.16.clone.1 | loop fusion | flops 30965760 | bytes 44237248 | tf_op jit(solution)/shard_map/while/body/eval_jaxpr/convert_element_type | solution.py:114
  986.4 18.9 %fusion.74 = bf16[32,20,2304]{2,1,0:T(8,128)(2,1)S(1)} fusion(f32[32,20,2304]{2,1,0:T(8,128)} %gather_fusion, f32[32,20,2304]{2,1,0:T(8,128)} %gather_fusion.1, f32[32,20,2304]{2,1,0:T(8,128)} %gather_fusion.2, f32[32,20,2304]{2,1,0:T(8,128)} %gather_fusion.3, f32[32,20,2304]{2,1,0:T(8,128)} %gather_fusion.4, f32[32,20,2304]{2,1,0:T(8,128)} %gather_fusion.5, ...), kind=kLoop, calls=%fused_computation.16.clone.1 | loop fusion | flops 30965760 | bytes 44237248 | tf_op jit(solution)/shard_map/while/body/eval_jaxpr/convert_element_type | solution.py:114
  1022.0 9.4 reshape_reshape_reshape.3
  1035.4 89.9 %all_gather.18 = f32[256,20,20]{2,1,0:T(8,128)} all-gather(f32[2,20,20]{2,1,0:T(8,128)S(1)} %copy.122), channel_id=1, replica_groups=mesh['row'=8,'col'=16] {'row','col'}, dimensions={0}, use_global_device_ids=true | all-gather | bytes 412800 | tf_op jit(solution)/shard_map/all_gather | solution.py:128
  (422 shorter events, 688.7 us)
Async XLA Ops:
  6.5 47.4 %all-gather.6.cloned.1.call-start = ((), (), s32[]{:S(2)}) async-start(), calls=%async_computation.2 | async-start | bytes 1392640 | tf_op jit(solution)/shard_map/all_gather | solution.py:65
  8.1 167.9 %all-gather.8.cloned.1.call-start = ((), (), s32[]{:S(2)}) async-start(), calls=%async_computation.3 | async-start | bytes 10321920 | tf_op jit(solution)/shard_map/all_gather | solution.py:76
  106.6 9.7 copy-start.1
  1022.0 13.2 %copy-start = (f32[2,20,20]{2,0,1:T(2,128)S(1)}, f32[2,20,20]{2,0,1:T(2,128)}, u32[]{:S(2)}) copy-start(f32[2,20,20]{2,0,1:T(2,128)} %param.17) | copy-start | bytes 9604
  1022.0 13.2 %copy-start.2 = (s32[2,2]{1,0:T(2,128)S(1)}, s32[2,2]{1,0:T(2,128)}, u32[]{:S(2)}) copy-start(s32[2,2]{1,0:T(2,128)} %param.16) | copy-start | bytes 52
  1031.4 93.9 %all-to-all-start = ((f32[16,8,1,2,1600]{4,1,3,2,0:T(8,128)}), f32[16,8,1,2,1600]{4,1,3,2,0:T(8,128)S(1)}, u32[]{:S(2)}, u32[]{:S(2)}) async-start(f32[16,8,1,2,1600]{4,1,3,2,0:T(8,128)} %bitcast.33), calls=%async_computation | async-start | bytes 3407872 | tf_op jit(solution)/shard_map/all_to_all | solution.py:26
  1126.1 10.0 all-to-all-start.1
Sparse Core Ops, SparseCore 0:
  9.5 44.3 all-gather.5
  56.9 55.0 all-gather.7
where the time goes:
time: 1160 us; the launch traced here: 1140 us
  local copies, waits for them, and re-layouts  564 us (49%)
  other arithmetic  215 us (19%)
  matrix products  144 us (12%)
  blocking collectives  140 us (12%)
  waiting for transfers between devices  48.2 us (4%)
  between operations  13.9 us (1%)
    gather x56, local copies, waits for them, and re-layouts, one_group(): picked = jnp.take(flat_parts, where_at, axis=0)  398 us
    convert_element_type x8, other arithmetic, one_group(): left = total.astype(jnp.bfloat16)  151 us
    all_gather x1, blocking collectives, shards(): every_amp = lax.all_gather(amplitudes, ('row', 'col'), axis=0, tiled=True)  89.9 us
    dot_general x8, matrix products, one_group(): jnp.einsum('tmak,tkw->tmaw', blocks, operator, preferred_element_type=jnp...  70.9 us
    dot_general x8, matrix products, one_group(): jnp.einsum('qamtk,qntbk->qnmab', left, partner, preferred_element_type=jn...  54 us
    all_gather x1, waiting for transfers between devices, shards(): lax.all_gather(coefficients, 'col', axis=0, tiled=True)  45.8 us
    reshape x8, local copies, waits for them, and re-layouts, one_group(): left = left.reshape(group_size, pno_count, 2, tile_cols, tile_size)  38.2 us
  transfers between devices with their start and end apart: 4, of which 2 were waited for; matrix products, arithmetic and copies ran while one was open for 6% of the time, Pallas kernels for 0%

commit v1 on v0

--- a/solution.py
+++ b/solution.py
@@ -125,7 +125,10 @@
     sectioned = sent_and_summed(sectioned, "col", 1)
     summed = sent_and_summed(sectioned, "row", 0)
     summed = summed.reshape(pair_dev, link_count, 2, pno_count, pno_count)
-    every_amp = lax.all_gather(amplitudes, ("row", "col"), axis=0, tiled=True)
+    size = lax.axis_size(("row", "col"))
+    pieces = jnp.stack([amplitudes for _ in range(size)])
+    pieces = lax.all_to_all(pieces, ("row", "col"), split_axis=0, concat_axis=0)
+    every_amp = jnp.concatenate(pieces, axis=0)
     nearby = jnp.take(every_amp, neighbours, axis=0)
     fock_part = summed[:, :, 0]
     over_part = summed[:, :, 1]

time: 1160 us -> 1110 us (0.957)
  blocking collectives: 140 us -> 49.5 us
  waiting for transfers between devices: 48.2 us -> 79.5 us
  local copies, waits for them, and re-layouts: 564 us -> 580 us
    all_gather x1 -> x0, blocking collectives: 89.9 us -> none  [shards(): every_amp = lax.all_gather(amplitudes, ('row', 'col'), axis=0, tiled=True)]
    reshape x8, local copies, waits for them, and re-layouts: 38.2 us -> 59.2 us  [one_group(): left = left.reshape(group_size, pno_count, 2, tile_cols, tile_size)]
    all_to_all x2, waiting for transfers between devices: 2.45 us -> 22.8 us  [sent_and_summed(): lax.all_to_all(tiles, axis, split_axis=0, concat_axis=0, tiled=True)]
    convert_element_type x8, other arithmetic: 151 us -> 165 us  [one_group(): left = total.astype(jnp.bfloat16)]
    and x32, other arithmetic: 13.6 us -> 0.27 us  [one_group(): picked = jnp.take(flat_parts, where_at, axis=0)]
    unnamed x12 -> x14, local copies, waits for them, and re-layouts: 18.8 us -> 27.8 us
  transfers between devices with their start and end apart: 4 -> 5, of which waited for: 2 -> 3; matrix products, arithmetic and copies ran while one was open for 6% -> 8% of each run, Pallas kernels for 0% -> 0%
where the time goes in v1:
time: 1110 us; the launch traced here: 1100 us
  local copies, waits for them, and re-layouts  580 us (52%)
  other arithmetic  213 us (19%)
  matrix products  145 us (13%)
  waiting for transfers between devices  79.5 us (7%)
  blocking collectives  49.5 us (4%)
  between operations  14 us (1%)
  starting transfers between devices  13 us (1%)
    gather x56, local copies, waits for them, and re-layouts, one_group(): picked = jnp.take(flat_parts, where_at, axis=0)  399 us
    convert_element_type x8, other arithmetic, one_group(): left = total.astype(jnp.bfloat16)  165 us
    dot_general x8, matrix products, one_group(): jnp.einsum('tmak,tkw->tmaw', blocks, operator, preferred_element_type=jnp...  71.4 us
    reshape x8, local copies, waits for them, and re-layouts, one_group(): left = left.reshape(group_size, pno_count, 2, tile_cols, tile_size)  59.2 us
    dot_general x8, matrix products, one_group(): jnp.einsum('qamtk,qntbk->qnmab', left, partner, preferred_element_type=jn...  54.3 us
    all_gather x1, waiting for transfers between devices, shards(): lax.all_gather(coefficients, 'col', axis=0, tiled=True)  45.7 us
    unnamed x14, local copies, waits for them, and re-layouts  27.8 us
    all_to_all x2, waiting for transfers between devices, sent_and_summed(): lax.all_to_all(tiles, axis, split_axis=0, concat_axis=0, tiled=True)  22.8 us
  transfers between devices with their start and end apart: 5, of which 3 were waited for; matrix products, arithmetic and copies ran while one was open for 8% of the time, Pallas kernels for 0%

profile of v1, /device:TPU:1, one launch (start us, length us, event | category | flops | bytes accessed | tf_op | source)
XLA Modules:
  0.0 1095.8 jit_solution(9345826332467137137)
XLA Ops:
  8.1 45.7 %all-gather.6.cloned.1.call-done = bf16[32,7,20,128]{3,1,2,0:T(8,128)(2,1)} async-done(((bf16[2,7,20,128]{3,1,2,0:T(8,128)(2,1)}), bf16[32,7,20,128]{3,1,2,0:T(8,128)(2,1)}) %all-gather.6.cloned.1.call-update) | async-done | bytes 1146896 | tf_op jit(solution)/shard_map/all_gather | solution.py:65
  57.5 17.6 %all-gather = s32[16,2,9]{2,1,0:T(2,128)S(1)} all-gather(s32[1,2,9]{2,1,0:T(2,128)S(1)} %add_bitcast_fusion), channel_id=1, replica_groups=mesh['row'=8,'col'=16] {'col'}, dimensions={0}, use_global_device_ids=true | all-gather | bytes 1224 | tf_op jit(solution)/shard_map/all_gather | solution.py:11
  75.3 21.1 %all-gather.1 = s32[8,32,7]{1,2,0:T(8,128)S(1)} all-gather(s32[1,32,7]{1,2,0:T(8,128)S(1)} %bitcast.153), channel_id=1, replica_groups=mesh['row'=8,'col'=16] {'row'}, dimensions={0}, use_global_device_ids=true | all-gather | bytes 8064 | tf_op jit(solution)/shard_map/all_gather | solution.py:77
  153.3 10.8 all-gather.2
  164.5 9.3 pad_maximum_fusion
  173.8 13.8 %copy.195 = bf16[256,7,20,128]{3,2,1,0:T(8,128)(2,1)} copy(bf16[256,7,20,128]{3,0,2,1:T(8,128)(2,1)} %all-gather.8.cloned.1.call-done) | data formatting | bytes 18350080 | tf_op jit(solution)/shard_map/vmap()/reshape;reshape | solution.py:45
  204.1 808.5 %while.12 = (s32[]{:T(128)}, f32[8,32,2,2,20,20]{5,4,3,2,0,1:T(8,128)}, s32[8,9,2]{0,2,1:T(2,128)S(1)}, s32[8,32,2]{1,2,0:T(2,128)S(1)}, bf16[8,9,2,20,128]{4,0,...) while((s32[]{:T(128)}, ...), condition=%wide.region_21.23_spmd, body=%wide.region_5.22_spmd.sunk | while | flops 622367552 | bytes 162233904 | solution.py:122
  206.5 8.9 fusion.72
  266.0 20.7 %fusion.74 = bf16[32,20,2304]{2,1,0:T(8,128)(2,1)} fusion(f32[32,20,2304]{2,1,0:T(8,128)} %gather_fusion, f32[32,20,2304]{2,1,0:T(8,128)} %gather_fusion.1, f32[32,20,2304]{2,1,0:T(8,128)} %gather_fusion.2, f32[32,20,2304]{2,1,0:T(8,128)} %gather_fusion.3, f32[32,20,2304]{2,1,0:T(8,128)} %gather_fusion.4, f32[32,20,2304]{2,1,0:T(8,128)} %gather_fusion.5, ...), kind=kLoop, calls=%fused_computation.16.clone.1 | loop fusion | flops 30965760 | bytes 44237248 | tf_op jit(solution)/shard_map/while/body/eval_jaxpr/convert_element_type | solution.py:114
  307.5 8.9 fusion.72
  366.9 20.7 %fusion.74 = bf16[32,20,2304]{2,1,0:T(8,128)(2,1)} fusion(f32[32,20,2304]{2,1,0:T(8,128)} %gather_fusion, f32[32,20,2304]{2,1,0:T(8,128)} %gather_fusion.1, f32[32,20,2304]{2,1,0:T(8,128)} %gather_fusion.2, f32[32,20,2304]{2,1,0:T(8,128)} %gather_fusion.3, f32[32,20,2304]{2,1,0:T(8,128)} %gather_fusion.4, f32[32,20,2304]{2,1,0:T(8,128)} %gather_fusion.5, ...), kind=kLoop, calls=%fused_computation.16.clone.1 | loop fusion | flops 30965760 | bytes 44237248 | tf_op jit(solution)/shard_map/while/body/eval_jaxpr/convert_element_type | solution.py:114
  408.5 8.9 fusion.72
  467.9 20.7 %fusion.74 = bf16[32,20,2304]{2,1,0:T(8,128)(2,1)} fusion(f32[32,20,2304]{2,1,0:T(8,128)} %gather_fusion, f32[32,20,2304]{2,1,0:T(8,128)} %gather_fusion.1, f32[32,20,2304]{2,1,0:T(8,128)} %gather_fusion.2, f32[32,20,2304]{2,1,0:T(8,128)} %gather_fusion.3, f32[32,20,2304]{2,1,0:T(8,128)} %gather_fusion.4, f32[32,20,2304]{2,1,0:T(8,128)} %gather_fusion.5, ...), kind=kLoop, calls=%fused_computation.16.clone.1 | loop fusion | flops 30965760 | bytes 44237248 | tf_op jit(solution)/shard_map/while/body/eval_jaxpr/convert_element_type | solution.py:114
  569.0 20.7 %fusion.74 = bf16[32,20,2304]{2,1,0:T(8,128)(2,1)} fusion(f32[32,20,2304]{2,1,0:T(8,128)} %gather_fusion, f32[32,20,2304]{2,1,0:T(8,128)} %gather_fusion.1, f32[32,20,2304]{2,1,0:T(8,128)} %gather_fusion.2, f32[32,20,2304]{2,1,0:T(8,128)} %gather_fusion.3, f32[32,20,2304]{2,1,0:T(8,128)} %gather_fusion.4, f32[32,20,2304]{2,1,0:T(8,128)} %gather_fusion.5, ...), kind=kLoop, calls=%fused_computation.16.clone.1 | loop fusion | flops 30965760 | bytes 44237248 | tf_op jit(solution)/shard_map/while/body/eval_jaxpr/convert_element_type | solution.py:114
  610.6 8.9 fusion.72
  670.0 20.7 %fusion.74 = bf16[32,20,2304]{2,1,0:T(8,128)(2,1)} fusion(f32[32,20,2304]{2,1,0:T(8,128)} %gather_fusion, f32[32,20,2304]{2,1,0:T(8,128)} %gather_fusion.1, f32[32,20,2304]{2,1,0:T(8,128)} %gather_fusion.2, f32[32,20,2304]{2,1,0:T(8,128)} %gather_fusion.3, f32[32,20,2304]{2,1,0:T(8,128)} %gather_fusion.4, f32[32,20,2304]{2,1,0:T(8,128)} %gather_fusion.5, ...), kind=kLoop, calls=%fused_computation.16.clone.1 | loop fusion | flops 30965760 | bytes 44237248 | tf_op jit(solution)/shard_map/while/body/eval_jaxpr/convert_element_type | solution.py:114
  711.6 8.9 fusion.72
  771.1 20.7 %fusion.74 = bf16[32,20,2304]{2,1,0:T(8,128)(2,1)} fusion(f32[32,20,2304]{2,1,0:T(8,128)} %gather_fusion, f32[32,20,2304]{2,1,0:T(8,128)} %gather_fusion.1, f32[32,20,2304]{2,1,0:T(8,128)} %gather_fusion.2, f32[32,20,2304]{2,1,0:T(8,128)} %gather_fusion.3, f32[32,20,2304]{2,1,0:T(8,128)} %gather_fusion.4, f32[32,20,2304]{2,1,0:T(8,128)} %gather_fusion.5, ...), kind=kLoop, calls=%fused_computation.16.clone.1 | loop fusion | flops 30965760 | bytes 44237248 | tf_op jit(solution)/shard_map/while/body/eval_jaxpr/convert_element_type | solution.py:114
  812.6 8.9 fusion.72
  872.1 20.7 %fusion.74 = bf16[32,20,2304]{2,1,0:T(8,128)(2,1)} fusion(f32[32,20,2304]{2,1,0:T(8,128)} %gather_fusion, f32[32,20,2304]{2,1,0:T(8,128)} %gather_fusion.1, f32[32,20,2304]{2,1,0:T(8,128)} %gather_fusion.2, f32[32,20,2304]{2,1,0:T(8,128)} %gather_fusion.3, f32[32,20,2304]{2,1,0:T(8,128)} %gather_fusion.4, f32[32,20,2304]{2,1,0:T(8,128)} %gather_fusion.5, ...), kind=kLoop, calls=%fused_computation.16.clone.1 | loop fusion | flops 30965760 | bytes 44237248 | tf_op jit(solution)/shard_map/while/body/eval_jaxpr/convert_element_type | solution.py:114
  973.1 20.7 %fusion.74 = bf16[32,20,2304]{2,1,0:T(8,128)(2,1)} fusion(f32[32,20,2304]{2,1,0:T(8,128)} %gather_fusion, f32[32,20,2304]{2,1,0:T(8,128)} %gather_fusion.1, f32[32,20,2304]{2,1,0:T(8,128)} %gather_fusion.2, f32[32,20,2304]{2,1,0:T(8,128)} %gather_fusion.3, f32[32,20,2304]{2,1,0:T(8,128)} %gather_fusion.4, f32[32,20,2304]{2,1,0:T(8,128)} %gather_fusion.5, ...), kind=kLoop, calls=%fused_computation.16.clone.1 | loop fusion | flops 30965760 | bytes 44237248 | tf_op jit(solution)/shard_map/while/body/eval_jaxpr/convert_element_type | solution.py:114
  1012.7 9.4 reshape_reshape_reshape.3
  1032.0 22.8 %all-to-all-done.1 = f32[16,8,1,2,1600]{4,1,3,2,0:T(8,128)} async-done(((f32[16,8,1,2,1600]{4,1,3,2,0:T(8,128)}), f32[16,8,1,2,1600]{4,1,3,2,0:T(8,128)}, u32[]{:S(2)}, u32[]{:S(2)}) %all-to-all-start.1) | async-done | bytes 1638432 | tf_op jit(solution)/shard_map/all_to_all | solution.py:26
  1061.5 11.0 %all-to-all-done = f32[128,1,800]{2,1,0:T(1,128)S(1)} async-done(((f32[128,1,800]{2,1,0:T(1,128)}), f32[128,1,800]{2,1,0:T(1,128)S(1)}, u32[]{:S(2)}, u32[]{:S(2)}) %all-to-all-start) | async-done | bytes 409632 | tf_op jit(solution)/shard_map/all_to_all | solution.py:130
  (428 shorter events, 700.0 us)
Async XLA Ops:
  6.5 1020.1 %copy-start = (f32[2,20,20]{2,0,1:T(2,128)S(1)}, f32[2,20,20]{2,0,1:T(2,128)}, u32[]{:S(2)}) copy-start(f32[2,20,20]{2,0,1:T(2,128)} %param.17) | copy-start | bytes 9604
  6.5 47.4 %all-gather.6.cloned.1.call-start = ((), (), s32[]{:S(2)}) async-start(), calls=%async_computation.3 | async-start | bytes 1392640 | tf_op jit(solution)/shard_map/all_gather | solution.py:65
  8.1 165.7 %all-gather.8.cloned.1.call-start = ((), (), s32[]{:S(2)}) async-start(), calls=%async_computation.4 | async-start | bytes 10321920 | tf_op jit(solution)/shard_map/all_gather | solution.py:76
  105.6 9.0 copy-start.1
  1022.1 37.1 %copy-start.2 = (s32[2,2]{1,0:T(2,128)S(1)}, s32[2,2]{1,0:T(2,128)}, u32[]{:S(2)}) copy-start(s32[2,2]{1,0:T(2,128)} %param.16) | copy-start | bytes 52
  1022.1 32.7 %all-to-all-start.1 = ((f32[16,8,1,2,1600]{4,1,3,2,0:T(8,128)}), f32[16,8,1,2,1600]{4,1,3,2,0:T(8,128)}, u32[]{:S(2)}, u32[]{:S(2)}) async-start(f32[16,8,1,2,1600]{4,1,3,2,0:T(8,128)} %bitcast.34), calls=%async_computation.1 | async-start | bytes 3407872 | tf_op jit(solution)/shard_map/all_to_all | solution.py:26
  1054.7 17.8 %all-to-all-start = ((f32[128,1,800]{2,1,0:T(1,128)}), f32[128,1,800]{2,1,0:T(1,128)S(1)}, u32[]{:S(2)}, u32[]{:S(2)}) async-start(f32[128,1,800]{2,1,0:T(1,128)} %reshape.309), calls=%async_computation | async-start | bytes 917504 | tf_op jit(solution)/shard_map/all_to_all | solution.py:130
  1072.5 14.5 %all-to-all-start.2 = ((f32[8,1,1,2,1600]{4,3,2,1,0:T(2,128)}), f32[8,1,1,2,1600]{4,3,2,1,0:T(2,128)S(1)}, u32[]{:S(2)}, u32[]{:S(2)}) async-start(f32[8,1,1,2,1600]{4,3,2,1,0:T(2,128)} %copy.172), calls=%async_computation.2 | async-start | bytes 212992 | tf_op jit(solution)/shard_map/all_to_all | solution.py:26
Sparse Core Ops, SparseCore 0:
  9.5 44.3 all-gather.5
  56.9 55.0 all-gather.7
